TPU v7x, 512 devices: a whole 4x8x8 slice. The times are simulated.
512 devices in a mesh: dp: 8 (over z_hi, x), expert: 64 (over y, z_lo, core).
Axes of the slice: x: 4, y: 8, z: 8 (z_hi: 2, z_lo: 4; z = z_hi * 4 + z_lo), core: 2. Of those that a mesh axis runs over, the one named last changes fastest.
Arguments:
- tokens: bfloat16 [65536, 1024], P(('dp', 'expert')), may hold values from -6 to 6
- cotangent: bfloat16 [65536, 1024], P(('dp', 'expert')), may hold values from -6 to 6
- pick_lists: int32 [8, 64, 128], P('dp'), may hold values from 0 to 8191, as said below
- combine: float32 [8, 64, 128], P('dp'), may hold values from 0.1 to 1
- w_gate: bfloat16 [64, 1024, 1024], P('expert', 'dp'), may hold values from -0.1875 to 0.1875
- w_up: bfloat16 [64, 1024, 1024], P('expert', 'dp'), may hold values from -0.1875 to 0.1875
- w_down: bfloat16 [64, 1024, 1024], P('expert', 'dp'), may hold values from -0.1875 to 0.1875
Outputs:
- layer_out: bfloat16 [65536, 1024], P(('dp', 'expert'))
- tokens_grad: bfloat16 [65536, 1024], P(('dp', 'expert'))
- grad_gate: bfloat16 [64, 1024, 1024], P('expert', 'dp')
- grad_up: bfloat16 [64, 1024, 1024], P('expert', 'dp')
- grad_down: bfloat16 [64, 1024, 1024], P('expert', 'dp')
Inputs may be any that keep to these rules, and one draw needn't show every extreme that they name: Each list pick_lists[r, e] names 128 distinct tokens of replica r. Token numbers j * 128 to (j + 1) * 128 - 1 are those of the device with index j on the expert axis; at most 4 picks of one expert in one replica fall among one device's tokens, and for every expert and replica exactly 4 fall among some device's.
All inputs are finite; a program needn't handle non-finite values.
Results may differ from a plain program's by a relative error of at most 0.013.
Values may be sent and summed in bfloat16 or wider, within the bound.
No kernel may reach another device: no remote copies, remote signals or barrier semaphores. Data moves between devices by JAX's collectives and lax.ppermute only.
A program may use at most 64 MiB of HBM per device.

v0:
```python
import jax
import jax.numpy as jnp
from jax import lax
from jax.sharding import PartitionSpec as P


def silu_parts(gate_pre):
    sigma_gate = jax.nn.sigmoid(gate_pre)
    return (gate_pre * sigma_gate, sigma_gate)


def project_hidden(row_block, gate_w, up_w):
    dims = (((1,), (1,)), ((), ()))
    gate_pre = lax.dot_general(row_block, gate_w, dims, preferred_element_type=jnp.float32)
    up_pre = lax.dot_general(row_block, up_w, dims, preferred_element_type=jnp.float32)
    silu_gate, sigma_gate = silu_parts(gate_pre)
    hidden = (silu_gate * up_pre).astype(jnp.bfloat16)
    return (gate_pre, up_pre, silu_gate, sigma_gate, hidden)


def backward_terms(grad_block, gate_pre, up_pre, silu_gate, sigma_gate, gate_w, up_w, down_w):
    dims = (((1,), (1,)), ((), ()))
    d_hidden = lax.dot_general(grad_block, down_w, dims, preferred_element_type=jnp.float32)
    d_gate = (d_hidden * up_pre * sigma_gate * (1.0 + gate_pre * (1.0 - sigma_gate))).astype(
        jnp.bfloat16
    )
    d_up = (d_hidden * silu_gate).astype(jnp.bfloat16)
    back_part = jnp.dot(d_gate, gate_w, preferred_element_type=jnp.float32) + jnp.dot(
        d_up, up_w, preferred_element_type=jnp.float32
    )
    return (d_gate, d_up, back_part)


def weight_grads(row_block, grad_block, hidden, d_gate, d_up):
    dims = (((0,), (0,)), ((), ()))
    grad_gate = lax.dot_general(d_gate, row_block, dims, preferred_element_type=jnp.float32).astype(
        jnp.bfloat16
    )
    grad_up = lax.dot_general(d_up, row_block, dims, preferred_element_type=jnp.float32).astype(
        jnp.bfloat16
    )
    grad_down = lax.dot_general(
        hidden, grad_block, dims, preferred_element_type=jnp.float32
    ).astype(jnp.bfloat16)
    return (grad_gate, grad_up, grad_down)


def per_device(tokens, cotangent, pick_lists, combine, w_gate, w_up, w_down):
    n_experts = lax.axis_size("expert")
    my_index = lax.axis_index("expert")
    tok_rows = tokens.shape[0]
    feat_width = tokens.shape[1]
    capacity = pick_lists.shape[2]
    slot_count = max(2, (2 * capacity + n_experts - 1) // n_experts)
    list_all = pick_lists[0]
    weight_all = combine[0]
    source_dev = list_all // tok_rows
    within_dev = list_all - source_dev * tok_rows
    is_mine = (source_dev == my_index).astype(jnp.int32)
    rank_mine = jnp.cumsum(is_mine, axis=1) - 1
    slot_ids = jnp.arange(slot_count, dtype=jnp.int32)
    select_mask = (is_mine[:, :, None] == 1) & (rank_mine[:, :, None] == slot_ids[None, None, :])
    select_int = select_mask.astype(jnp.int32)
    flat_row = jnp.sum(select_int * within_dev[:, :, None], axis=1).reshape(-1)
    flat_valid = (jnp.sum(select_int, axis=1) > 0).reshape(-1)
    flat_weight = jnp.sum(jnp.where(select_mask, weight_all[:, :, None], 0.0), axis=1).reshape(-1)
    slot_shape = (n_experts, slot_count, feat_width)
    row_send = jnp.where(
        flat_valid[:, None], jnp.take(tokens, flat_row, axis=0), jnp.zeros((), jnp.bfloat16)
    ).reshape(slot_shape)
    cot_rows = jnp.take(cotangent, flat_row, axis=0).astype(jnp.float32)
    grad_send = (
        jnp.where(flat_valid[:, None], flat_weight[:, None] * cot_rows, 0.0)
        .astype(jnp.bfloat16)
        .reshape(slot_shape)
    )
    own_source = lax.dynamic_index_in_dim(source_dev, my_index, 0, keepdims=False)
    order_ids = jnp.arange(capacity, dtype=jnp.int32)
    earlier = order_ids[:, None] > order_ids[None, :]
    same_source = own_source[:, None] == own_source[None, :]
    own_rank = jnp.sum((earlier & same_source).astype(jnp.int32), axis=1)
    position = own_source * slot_count + own_rank

    def compact(received):
        return jnp.take(received.reshape(n_experts * slot_count, feat_width), position, axis=0)

    def expand(result_rows):
        empty_slots = jnp.zeros((n_experts * slot_count, feat_width), jnp.bfloat16)
        return empty_slots.at[position].set(result_rows.astype(jnp.bfloat16)).reshape(slot_shape)

    gate_w = w_gate[0]
    up_w = w_up[0]
    down_w = w_down[0]
    recv_rows = lax.all_to_all(row_send, "expert", split_axis=0, concat_axis=0, tiled=True)
    row_block = lax.all_gather(compact(recv_rows), "dp", axis=0, tiled=True)
    gate_pre, up_pre, silu_gate, sigma_gate, hidden = project_hidden(row_block, gate_w, up_w)
    out_part = jnp.dot(hidden, down_w, preferred_element_type=jnp.float32)
    out_rows = lax.psum_scatter(
        out_part.astype(jnp.bfloat16), "dp", scatter_dimension=0, tiled=True
    ).astype(jnp.float32)
    out_slots = lax.all_to_all(expand(out_rows), "expert", split_axis=0, concat_axis=0, tiled=True)
    recv_grads = lax.all_to_all(grad_send, "expert", split_axis=0, concat_axis=0, tiled=True)
    grad_block = lax.all_gather(compact(recv_grads), "dp", axis=0, tiled=True)
    d_gate, d_up, back_part = backward_terms(
        grad_block, gate_pre, up_pre, silu_gate, sigma_gate, gate_w, up_w, down_w
    )
    back_rows = lax.psum_scatter(
        back_part.astype(jnp.bfloat16), "dp", scatter_dimension=0, tiled=True
    ).astype(jnp.float32)
    back_slots = lax.all_to_all(
        expand(back_rows), "expert", split_axis=0, concat_axis=0, tiled=True
    )
    grad_gate, grad_up, grad_down = weight_grads(row_block, grad_block, hidden, d_gate, d_up)
    out_flat = jnp.where(
        flat_valid[:, None],
        flat_weight[:, None] * out_slots.reshape(-1, feat_width).astype(jnp.float32),
        0.0,
    )
    layer_out = (
        jnp.zeros((tok_rows, feat_width), jnp.float32)
        .at[flat_row]
        .add(out_flat)
        .astype(jnp.bfloat16)
    )
    back_flat = jnp.where(
        flat_valid[:, None], back_slots.reshape(-1, feat_width).astype(jnp.float32), 0.0
    )
    tokens_grad = (
        jnp.zeros((tok_rows, feat_width), jnp.float32)
        .at[flat_row]
        .add(back_flat)
        .astype(jnp.bfloat16)
    )
    return (layer_out, tokens_grad, grad_gate[None], grad_up[None], grad_down[None])


def solution(mesh):
    placed = (
        P(("dp", "expert"), None),
        P(("dp", "expert"), None),
        P("dp", None, None),
        P("dp", None, None),
        P("expert", "dp", None),
        P("expert", "dp", None),
        P("expert", "dp", None),
    )
    return jax.shard_map(
        per_device,
        mesh=mesh,
        in_specs=placed,
        out_specs=(
            P(("dp", "expert"), None),
            P(("dp", "expert"), None),
            P("expert", "dp", None),
            P("expert", "dp", None),
            P("expert", "dp", None),
        ),
        check_vma=False,
    )
```

profile of v0, /device:TPU:1, one launch (start us, length us, event | category | flops | bytes accessed | tf_op | source)
XLA Modules:
  0.0 480.7 jit_solution(4581792306209189560)
XLA Ops:
  7.2 0.8 broadcast_compare_fusion
  8.0 0.3 reduce_window_sum.11
  8.3 0.8 add_select_fusion
  9.1 0.2 convert_reduce_fusion
  9.6 0.9 select_reduce_fusion
  10.6 0.1 gt.25
  10.9 1.2 gather_fusion.2
  12.1 0.3 select_convert_fusion
  12.4 1.0 reshape.203
  13.4 14.6 %all-to-all-start.2 = ((bf16[64,4,1024]{2,1,0:T(4,128)(2,1)}), bf16[64,4,1024]{2,1,0:T(4,128)(2,1)S(1)}, u32[]{:S(2)}, u32[]{:S(2)}) async-start(bf16[64,4,1024]{2,1,0:T(4,128)(2,1)} %reshape.203), calls=%async_computation.3 | async-start | bytes 1048576 | tf_op jit(solution)/shard_map/all_to_all | solution.py:102
  28.0 1.2 gather_fusion
  29.1 0.1 select_select_fusion
  29.3 1.0 reshape.200
  30.3 15.4 %all-to-all-done.2 = bf16[64,4,1024]{2,1,0:T(4,128)(2,1)S(1)} async-done(((bf16[64,4,1024]{2,1,0:T(4,128)(2,1)}), bf16[64,4,1024]{2,1,0:T(4,128)(2,1)S(1)}, u32[]{:S(2)}, u32[]{:S(2)}) %all-to-all-start.2) | async-done | bytes 524320 | tf_op jit(solution)/shard_map/all_to_all | solution.py:102
  45.6 5.6 %all-to-all-start = ((bf16[64,4,1024]{2,1,0:T(4,128)(2,1)}), bf16[64,4,1024]{2,1,0:T(4,128)(2,1)S(1)}, u32[]{:S(2)}, u32[]{:S(2)}) async-start(bf16[64,4,1024]{2,1,0:T(4,128)(2,1)} %reshape.200), calls=%async_computation | async-start | bytes 1048576 | tf_op jit(solution)/shard_map/all_to_all | solution.py:94
  51.3 0.2 convert_reduce_fusion.1
  51.5 0.1 reshape.204
  51.6 0.9 gather_fusion.3
  52.5 16.4 %all-to-all-done = bf16[64,4,1024]{2,1,0:T(4,128)(2,1)S(1)} async-done(((bf16[64,4,1024]{2,1,0:T(4,128)(2,1)}), bf16[64,4,1024]{2,1,0:T(4,128)(2,1)S(1)}, u32[]{:S(2)}, u32[]{:S(2)}) %all-to-all-start) | async-done | bytes 524320 | tf_op jit(solution)/shard_map/all_to_all | solution.py:94
  68.9 0.1 reshape.201
  69.1 0.9 gather_fusion.1
  69.9 0.9 broadcast_select_fusion
  70.9 0.7 all-gather.5.cloned.1.call-update
  71.7 78.6 %all-gather.3.cloned.1.call-done = bf16[1024,1024]{1,0:T(8,128)(2,1)} async-done(((bf16[128,1024]{1,0:T(8,128)(2,1)}), bf16[1024,1024]{1,0:T(8,128)(2,1)}) %all-gather.3.cloned.1.call-update) | async-done | bytes 2097168 | tf_op jit(solution)/shard_map/all_gather | solution.py:95
  150.3 3.3 fusion.18
  153.6 1.5 fusion.22
  155.1 76.9 %all-gather.5.cloned.1.call-done = bf16[1024,1024]{1,0:T(8,128)(2,1)} async-done(((bf16[128,1024]{1,0:T(8,128)(2,1)}), bf16[1024,1024]{1,0:T(8,128)(2,1)}) %all-gather.5.cloned.1.call-update) | async-done | bytes 2097168 | tf_op jit(solution)/shard_map/all_gather | solution.py:103
  232.0 2.6 multiply_convert_fusion
  234.7 0.7 copy-done.6
  235.3 2.0 convolution_convert_fusion
  237.4 0.7 fusion.20
  238.1 2.0 add_convert_fusion
  240.2 94.4 %reduce-scatter.3.cloned.1.call-done = bf16[128,1024]{1,0:T(8,128)(2,1)} async-done(((bf16[1024,1024]{1,0:T(8,128)(2,1)}), bf16[128,1024]{1,0:T(8,128)(2,1)}) %reduce-scatter.3.cloned.1.call-update) | async-done | bytes 262160 | tf_op jit(solution)/shard_map/reduce_scatter | solution.py:98
  334.6 1.7 scatter_custom_fusion
  336.3 1.0 reshape.202
  337.3 10.0 %all-to-all-start.1 = ((bf16[64,4,1024]{2,1,0:T(4,128)(2,1)}), bf16[64,4,1024]{2,1,0:T(4,128)(2,1)S(1)}, u32[]{:S(2)}, u32[]{:S(2)}) async-start(bf16[64,4,1024]{2,1,0:T(4,128)(2,1)} %reshape.202), calls=%async_computation.2 | async-start | bytes 1048576 | tf_op jit(solution)/shard_map/all_to_all | solution.py:101
  347.3 92.8 %reduce-scatter.5.cloned.1.call-done = bf16[128,1024]{1,0:T(8,128)(2,1)} async-done(((bf16[1024,1024]{1,0:T(8,128)(2,1)}), bf16[128,1024]{1,0:T(8,128)(2,1)}) %reduce-scatter.5.cloned.1.call-update) | async-done | bytes 262160 | tf_op jit(solution)/shard_map/reduce_scatter | solution.py:107
  440.1 1.7 scatter_custom_fusion.2
  441.8 1.0 reshape.205
  442.8 9.9 %all-to-all-start.3 = ((bf16[64,4,1024]{2,1,0:T(4,128)(2,1)}), bf16[64,4,1024]{2,1,0:T(4,128)(2,1)S(1)}, u32[]{:S(2)}, u32[]{:S(2)}) async-start(bf16[64,4,1024]{2,1,0:T(4,128)(2,1)} %reshape.205), calls=%async_computation.5 | async-start | bytes 1048576 | tf_op jit(solution)/shard_map/all_to_all | solution.py:110
  452.9 2.9 fusion.2
  455.8 1.2 fusion.1
  457.0 1.2 fusion
  458.2 2.9 scatter_custom_fusion.1
  461.2 0.7 convert_element_type.76
  461.9 8.5 %all-to-all-done.3 = bf16[64,4,1024]{2,1,0:T(4,128)(2,1)S(1)} async-done(((bf16[64,4,1024]{2,1,0:T(4,128)(2,1)}), bf16[64,4,1024]{2,1,0:T(4,128)(2,1)S(1)}, u32[]{:S(2)}, u32[]{:S(2)}) %all-to-all-start.3) | async-done | bytes 524320 | tf_op jit(solution)/shard_map/all_to_all | solution.py:110
  470.5 2.9 scatter_custom_fusion.3
  473.4 0.7 convert_element_type.84
  (46 shorter events, 1.1 us)
Async XLA Ops:
  7.2 224.8 %copy-start = (bf16[1,128,1024]{2,1,0:T(8,128)(2,1)S(1)}, bf16[1,128,1024]{2,1,0:T(8,128)(2,1)}, u32[]{:S(2)}) copy-start(bf16[1,128,1024]{2,1,0:T(8,128)(2,1)} %param.17) | copy-start | bytes 786436
  7.2 3.7 copy-start.1
  12.1 15.9 %copy-start.2 = (bf16[128,1024]{1,0:T(8,128)(2,1)S(1)}, bf16[128,1024]{1,0:T(8,128)(2,1)}, u32[]{:S(2)}) copy-start(bf16[128,1024]{1,0:T(8,128)(2,1)} %param.11) | copy-start | bytes 786436
  13.4 32.3 %all-to-all-start.2 = ((bf16[64,4,1024]{2,1,0:T(4,128)(2,1)}), bf16[64,4,1024]{2,1,0:T(4,128)(2,1)S(1)}, u32[]{:S(2)}, u32[]{:S(2)}) async-start(bf16[64,4,1024]{2,1,0:T(4,128)(2,1)} %reshape.203), calls=%async_computation.3 | async-start | bytes 1048576 | tf_op jit(solution)/shard_map/all_to_all | solution.py:102
  45.6 23.3 %all-to-all-start = ((bf16[64,4,1024]{2,1,0:T(4,128)(2,1)}), bf16[64,4,1024]{2,1,0:T(4,128)(2,1)S(1)}, u32[]{:S(2)}, u32[]{:S(2)}) async-start(bf16[64,4,1024]{2,1,0:T(4,128)(2,1)} %reshape.200), calls=%async_computation | async-start | bytes 1048576 | tf_op jit(solution)/shard_map/all_to_all | solution.py:94
  51.2 99.1 %all-gather.3.cloned.1.call-start = ((), (), s32[]{:S(2)}) async-start(), calls=%async_computation.6 | async-start | bytes 2359296 | tf_op jit(solution)/shard_map/all_gather | solution.py:95
  69.0 81.2 %copy-start.10 = (bf16[1,128,1024]{2,1,0:T(8,128)(2,1)S(1)}, bf16[1,128,1024]{2,1,0:T(8,128)(2,1)}, u32[]{:S(2)}) copy-start(bf16[1,128,1024]{2,1,0:T(8,128)(2,1)} %param.16) | copy-start | bytes 786436
  69.9 83.6 %copy-start.7 = (bf16[1,128,1024]{2,1,0:T(8,128)(2,1)S(1)}, bf16[1,128,1024]{2,1,0:T(8,128)(2,1)}, u32[]{:S(2)}) copy-start(bf16[1,128,1024]{2,1,0:T(8,128)(2,1)} %param.15) | copy-start | bytes 786436
  70.9 161.1 %all-gather.5.cloned.1.call-start = ((), (), s32[]{:S(2)}) async-start(), calls=%async_computation.8 | async-start | bytes 2359296 | tf_op jit(solution)/shard_map/all_gather | solution.py:103
  71.6 263.0 %reduce-scatter.3.cloned.1.call-start = ((), (), s32[]{:S(2)}) async-start(), calls=%async_computation.7 | async-start | bytes 2359296 | tf_op jit(solution)/shard_map/reduce_scatter | solution.py:98
  150.3 3.3 copy-start.3
  234.6 0.7 copy-start.6
  234.6 2.8 copy-start.4
  234.6 3.5 copy-start.8
  237.4 202.7 %reduce-scatter.5.cloned.1.call-start = ((), (), s32[]{:S(2)}) async-start(), calls=%async_computation.9 | async-start | bytes 2359296 | tf_op jit(solution)/shard_map/reduce_scatter | solution.py:107
  337.3 105.5 %all-to-all-start.1 = ((bf16[64,4,1024]{2,1,0:T(4,128)(2,1)}), bf16[64,4,1024]{2,1,0:T(4,128)(2,1)S(1)}, u32[]{:S(2)}, u32[]{:S(2)}) async-start(bf16[64,4,1024]{2,1,0:T(4,128)(2,1)} %reshape.202), calls=%async_computation.2 | async-start | bytes 1048576 | tf_op jit(solution)/shard_map/all_to_all | solution.py:101
  442.8 27.6 %all-to-all-start.3 = ((bf16[64,4,1024]{2,1,0:T(4,128)(2,1)}), bf16[64,4,1024]{2,1,0:T(4,128)(2,1)S(1)}, u32[]{:S(2)}, u32[]{:S(2)}) async-start(bf16[64,4,1024]{2,1,0:T(4,128)(2,1)} %reshape.205), calls=%async_computation.5 | async-start | bytes 1048576 | tf_op jit(solution)/shard_map/all_to_all | solution.py:110
  452.8 3.0 copy-start.9
  452.9 4.1 copy-start.5
Sparse Core Ops, SparseCore 0:
  71.0 79.2 all-gather.2
  154.1 77.8 all-gather.4
  237.5 97.0 reduce-scatter.2
  339.1 100.9 reduce-scatter.4
where the time goes:
time: 481 us
  waiting for transfers between devices  384 us (80%)
  starting transfers between devices  40.2 us (8%)
  matrix products  17.4 us (4%)
  between operations  14.1 us (3%)
  local copies, waits for them, and re-layouts  13.3 us (3%)
  other arithmetic  11.8 us (2%)
    reduce_scatter x1, waiting for transfers between devices, per_device(): lax.psum_scatter(out_part.astype(jnp.bfloat16), 'dp', scatter_dimension=0...  94.4 us
    reduce_scatter x1, waiting for transfers between devices, per_device(): lax.psum_scatter(back_part.astype(jnp.bfloat16), 'dp', scatter_dimension=...  92.8 us
    all_gather x1, waiting for transfers between devices, per_device(): row_block = lax.all_gather(compact(recv_rows), 'dp', axis=0, tiled=True)  78.6 us
    all_gather x1, waiting for transfers between devices, per_device(): grad_block = lax.all_gather(compact(recv_grads), 'dp', axis=0, tiled=True)  76.9 us
    all_to_all x1, waiting for transfers between devices, per_device(): lax.all_to_all(row_send, 'expert', split_axis=0, concat_axis=0, tiled=True)  16.4 us
    all_to_all x1, waiting for transfers between devices, per_device(): lax.all_to_all(grad_send, 'expert', split_axis=0, concat_axis=0, tiled=True)  15.4 us
    all_to_all x1, starting transfers between devices, per_device(): lax.all_to_all(grad_send, 'expert', split_axis=0, concat_axis=0, tiled=True)  14.6 us
    all_to_all x1, starting transfers between devices, per_device(): lax.all_to_all(expand(out_rows), 'expert', split_axis=0, concat_axis=0, t...  9.97 us
  transfers between devices with their start and end apart: 8, of which 7 were waited for; matrix products, arithmetic and copies ran while one was open for 5% of the time, Pallas kernels for 0%

commit v1 on v0

--- a/solution.py
+++ b/solution.py
@@ -92,7 +92,11 @@
     up_w = w_up[0]
     down_w = w_down[0]
     recv_rows = lax.all_to_all(row_send, "expert", split_axis=0, concat_axis=0, tiled=True)
-    row_block = lax.all_gather(compact(recv_rows), "dp", axis=0, tiled=True)
+    part = compact(recv_rows)
+    n_dev = lax.axis_size("dp")
+    pieces = jnp.stack([part for _ in range(n_dev)])
+    pieces = lax.all_to_all(pieces, "dp", split_axis=0, concat_axis=0)
+    row_block = jnp.concatenate(pieces, axis=0)
     gate_pre, up_pre, silu_gate, sigma_gate, hidden = project_hidden(row_block, gate_w, up_w)
     out_part = jnp.dot(hidden, down_w, preferred_element_type=jnp.float32)
     out_rows = lax.psum_scatter(

time: 481 us -> 432 us (0.90)
  waiting for transfers between devices: 384 us -> 325 us
  starting transfers between devices: 40.2 us -> 50.1 us
    all_gather x1 -> x0, waiting for transfers between devices: 78.6 us -> none  [per_device(): row_block = lax.all_gather(compact(recv_rows), 'dp', axis=0, tiled=True)]
    all_to_all x0 -> x1, waiting for transfers between devices: none -> 34.3 us  [per_device(): pieces = lax.all_to_all(pieces, 'dp', split_axis=0, concat_axis=0)]
    all_gather x1, waiting for transfers between devices: 76.9 us -> 61.9 us  [per_device(): grad_block = lax.all_gather(compact(recv_grads), 'dp', axis=0, tiled=True)]
    all_to_all x0 -> x1, starting transfers between devices: none -> 9.9 us  [per_device(): pieces = lax.all_to_all(pieces, 'dp', split_axis=0, concat_axis=0)]
where the time goes in v1:
time: 432 us; the launch traced here: 431 us
  waiting for transfers between devices  325 us (75%)
  starting transfers between devices  50.1 us (12%)
  matrix products  15 us (3%)
  local copies, waits for them, and re-layouts  14.9 us (3%)
  between operations  14.1 us (3%)
  other arithmetic  11.7 us (3%)
    reduce_scatter x1, waiting for transfers between devices, per_device(): lax.psum_scatter(out_part.astype(jnp.bfloat16), 'dp', scatter_dimension=0...  94.7 us
    reduce_scatter x1, waiting for transfers between devices, per_device(): lax.psum_scatter(back_part.astype(jnp.bfloat16), 'dp', scatter_dimension=...  92.6 us
    all_gather x1, waiting for transfers between devices, per_device(): grad_block = lax.all_gather(compact(recv_grads), 'dp', axis=0, tiled=True)  61.9 us
    all_to_all x1, waiting for transfers between devices, per_device(): pieces = lax.all_to_all(pieces, 'dp', split_axis=0, concat_axis=0)  34.3 us
    all_to_all x1, waiting for transfers between devices, per_device(): lax.all_to_all(row_send, 'expert', split_axis=0, concat_axis=0, tiled=True)  16.5 us
    all_to_all x1, waiting for transfers between devices, per_device(): lax.all_to_all(grad_send, 'expert', split_axis=0, concat_axis=0, tiled=True)  15.4 us
    all_to_all x1, starting transfers between devices, per_device(): lax.all_to_all(grad_send, 'expert', split_axis=0, concat_axis=0, tiled=True)  14.6 us
    all_to_all x1, starting transfers between devices, per_device(): lax.all_to_all(expand(back_rows), 'expert', split_axis=0, concat_axis=0,...  9.98 us
  transfers between devices with their start and end apart: 8, of which 7 were waited for; matrix products, arithmetic and copies ran while one was open for 5% of the time, Pallas kernels for 0%

profile of v1, /device:TPU:1, one launch (start us, length us, event | category | flops | bytes accessed | tf_op | source)
XLA Modules:
  0.0 431.1 jit_solution(11905214743651437053)
XLA Ops:
  7.2 0.8 broadcast_compare_fusion
  8.0 0.3 reduce_window_sum.11
  8.3 0.8 add_select_fusion
  9.1 0.2 convert_reduce_fusion
  9.6 0.9 select_reduce_fusion
  10.9 1.2 gather_fusion.2
  12.1 0.3 select_convert_fusion
  12.4 1.0 reshape.209
  13.4 14.6 %all-to-all-start.3 = ((bf16[64,4,1024]{2,1,0:T(4,128)(2,1)}), bf16[64,4,1024]{2,1,0:T(4,128)(2,1)S(1)}, u32[]{:S(2)}, u32[]{:S(2)}) async-start(bf16[64,4,1024]{2,1,0:T(4,128)(2,1)} %reshape.209), calls=%async_computation.4 | async-start | bytes 1048576 | tf_op jit(solution)/shard_map/all_to_all | solution.py:106
  28.0 1.2 gather_fusion
  29.1 0.1 select_select_fusion
  29.3 1.0 reshape.205
  30.3 15.4 %all-to-all-done.3 = bf16[64,4,1024]{2,1,0:T(4,128)(2,1)S(1)} async-done(((bf16[64,4,1024]{2,1,0:T(4,128)(2,1)}), bf16[64,4,1024]{2,1,0:T(4,128)(2,1)S(1)}, u32[]{:S(2)}, u32[]{:S(2)}) %all-to-all-start.3) | async-done | bytes 524320 | tf_op jit(solution)/shard_map/all_to_all | solution.py:106
  45.6 5.6 %all-to-all-start = ((bf16[64,4,1024]{2,1,0:T(4,128)(2,1)}), bf16[64,4,1024]{2,1,0:T(4,128)(2,1)S(1)}, u32[]{:S(2)}, u32[]{:S(2)}) async-start(bf16[64,4,1024]{2,1,0:T(4,128)(2,1)} %reshape.205), calls=%async_computation | async-start | bytes 1048576 | tf_op jit(solution)/shard_map/all_to_all | solution.py:94
  51.2 0.2 convert_reduce_fusion.1
  51.5 0.1 reshape.210
  51.6 0.9 gather_fusion.3
  52.4 16.5 %all-to-all-done = bf16[64,4,1024]{2,1,0:T(4,128)(2,1)S(1)} async-done(((bf16[64,4,1024]{2,1,0:T(4,128)(2,1)}), bf16[64,4,1024]{2,1,0:T(4,128)(2,1)S(1)}, u32[]{:S(2)}, u32[]{:S(2)}) %all-to-all-start) | async-done | bytes 524320 | tf_op jit(solution)/shard_map/all_to_all | solution.py:94
  69.0 0.9 gather_fusion.1
  69.9 0.8 broadcast_select_fusion
  70.7 1.6 stack.2
  72.3 9.9 %all-to-all-start.1 = ((bf16[8,128,1024]{2,1,0:T(8,128)(2,1)}), bf16[8,128,1024]{2,1,0:T(8,128)(2,1)S(1)}, u32[]{:S(2)}, u32[]{:S(2)}) async-start(bf16[8,128,1024]{2,1,0:T(8,128)(2,1)} %stack.2), calls=%async_computation.1 | async-start | bytes 4194304 | tf_op jit(solution)/shard_map/all_to_all | solution.py:98
  82.2 0.7 all-gather.2.cloned.1.call-update
  83.0 34.3 %all-to-all-done.1 = bf16[8,128,1024]{2,1,0:T(8,128)(2,1)S(1)} async-done(((bf16[8,128,1024]{2,1,0:T(8,128)(2,1)}), bf16[8,128,1024]{2,1,0:T(8,128)(2,1)S(1)}, u32[]{:S(2)}, u32[]{:S(2)}) %all-to-all-start.1) | async-done | bytes 2097184 | tf_op jit(solution)/shard_map/all_to_all | solution.py:98
  117.3 1.5 fusion.18
  118.8 1.5 fusion.22
  120.3 61.9 %all-gather.2.cloned.1.call-done = bf16[1024,1024]{1,0:T(8,128)(2,1)} async-done(((bf16[128,1024]{1,0:T(8,128)(2,1)}), bf16[1024,1024]{1,0:T(8,128)(2,1)}) %all-gather.2.cloned.1.call-update) | async-done | bytes 2097168 | tf_op jit(solution)/shard_map/all_gather | solution.py:107
  182.2 2.6 multiply_convert_fusion
  184.8 0.7 copy-done.4
  185.5 2.0 convolution_convert_fusion
  187.6 0.7 fusion.20
  188.3 2.0 add_convert_fusion
  190.3 94.7 %reduce-scatter.3.cloned.1.call-done = bf16[128,1024]{1,0:T(8,128)(2,1)} async-done(((bf16[1024,1024]{1,0:T(8,128)(2,1)}), bf16[128,1024]{1,0:T(8,128)(2,1)}) %reduce-scatter.3.cloned.1.call-update) | async-done | bytes 262160 | tf_op jit(solution)/shard_map/reduce_scatter | solution.py:102
  285.1 1.7 scatter_custom_fusion
  286.8 1.0 reshape.208
  287.8 10.0 %all-to-all-start.2 = ((bf16[64,4,1024]{2,1,0:T(4,128)(2,1)}), bf16[64,4,1024]{2,1,0:T(4,128)(2,1)S(1)}, u32[]{:S(2)}, u32[]{:S(2)}) async-start(bf16[64,4,1024]{2,1,0:T(4,128)(2,1)} %reshape.208), calls=%async_computation.3 | async-start | bytes 1048576 | tf_op jit(solution)/shard_map/all_to_all | solution.py:105
  297.8 92.6 %reduce-scatter.5.cloned.1.call-done = bf16[128,1024]{1,0:T(8,128)(2,1)} async-done(((bf16[1024,1024]{1,0:T(8,128)(2,1)}), bf16[128,1024]{1,0:T(8,128)(2,1)}) %reduce-scatter.5.cloned.1.call-update) | async-done | bytes 262160 | tf_op jit(solution)/shard_map/reduce_scatter | solution.py:111
  390.4 1.7 scatter_custom_fusion.2
  392.2 1.0 reshape.211
  393.1 10.0 %all-to-all-start.4 = ((bf16[64,4,1024]{2,1,0:T(4,128)(2,1)}), bf16[64,4,1024]{2,1,0:T(4,128)(2,1)S(1)}, u32[]{:S(2)}, u32[]{:S(2)}) async-start(bf16[64,4,1024]{2,1,0:T(4,128)(2,1)} %reshape.211), calls=%async_computation.6 | async-start | bytes 1048576 | tf_op jit(solution)/shard_map/all_to_all | solution.py:114
  403.3 2.3 fusion.1
  405.6 1.2 fusion
  406.7 1.2 fusion.2
  408.0 2.9 scatter_custom_fusion.1
  410.9 0.7 convert_element_type.76
  411.7 9.2 %all-to-all-done.4 = bf16[64,4,1024]{2,1,0:T(4,128)(2,1)S(1)} async-done(((bf16[64,4,1024]{2,1,0:T(4,128)(2,1)}), bf16[64,4,1024]{2,1,0:T(4,128)(2,1)S(1)}, u32[]{:S(2)}, u32[]{:S(2)}) %all-to-all-start.4) | async-done | bytes 524320 | tf_op jit(solution)/shard_map/all_to_all | solution.py:114
  420.9 2.9 scatter_custom_fusion.3
  423.8 0.7 convert_element_type.84
  (46 shorter events, 1.3 us)
Async XLA Ops:
  7.2 175.0 %copy-start = (bf16[1,128,1024]{2,1,0:T(8,128)(2,1)S(1)}, bf16[1,128,1024]{2,1,0:T(8,128)(2,1)}, u32[]{:S(2)}) copy-start(bf16[1,128,1024]{2,1,0:T(8,128)(2,1)} %param.17) | copy-start | bytes 786436
  7.2 3.7 copy-start.1
  12.1 15.8 %copy-start.2 = (bf16[128,1024]{1,0:T(8,128)(2,1)S(1)}, bf16[128,1024]{1,0:T(8,128)(2,1)}, u32[]{:S(2)}) copy-start(bf16[128,1024]{1,0:T(8,128)(2,1)} %param.11) | copy-start | bytes 786436
  13.4 32.3 %all-to-all-start.3 = ((bf16[64,4,1024]{2,1,0:T(4,128)(2,1)}), bf16[64,4,1024]{2,1,0:T(4,128)(2,1)S(1)}, u32[]{:S(2)}, u32[]{:S(2)}) async-start(bf16[64,4,1024]{2,1,0:T(4,128)(2,1)} %reshape.209), calls=%async_computation.4 | async-start | bytes 1048576 | tf_op jit(solution)/shard_map/all_to_all | solution.py:106
  45.6 23.3 %all-to-all-start = ((bf16[64,4,1024]{2,1,0:T(4,128)(2,1)}), bf16[64,4,1024]{2,1,0:T(4,128)(2,1)S(1)}, u32[]{:S(2)}, u32[]{:S(2)}) async-start(bf16[64,4,1024]{2,1,0:T(4,128)(2,1)} %reshape.205), calls=%async_computation | async-start | bytes 1048576 | tf_op jit(solution)/shard_map/all_to_all | solution.py:94
  72.3 45.0 %copy-start.10 = (bf16[1,128,1024]{2,1,0:T(8,128)(2,1)S(1)}, bf16[1,128,1024]{2,1,0:T(8,128)(2,1)}, u32[]{:S(2)}) copy-start(bf16[1,128,1024]{2,1,0:T(8,128)(2,1)} %param.16) | copy-start | bytes 786436
  72.3 45.0 %all-to-all-start.1 = ((bf16[8,128,1024]{2,1,0:T(8,128)(2,1)}), bf16[8,128,1024]{2,1,0:T(8,128)(2,1)S(1)}, u32[]{:S(2)}, u32[]{:S(2)}) async-start(bf16[8,128,1024]{2,1,0:T(8,128)(2,1)} %stack.2), calls=%async_computation.1 | async-start | bytes 4194304 | tf_op jit(solution)/shard_map/all_to_all | solution.py:98
  82.2 36.6 %copy-start.8 = (bf16[1,128,1024]{2,1,0:T(8,128)(2,1)S(1)}, bf16[1,128,1024]{2,1,0:T(8,128)(2,1)}, u32[]{:S(2)}) copy-start(bf16[1,128,1024]{2,1,0:T(8,128)(2,1)} %param.15) | copy-start | bytes 786436
  82.2 100.0 %all-gather.2.cloned.1.call-start = ((), (), s32[]{:S(2)}) async-start(), calls=%async_computation.8 | async-start | bytes 2359296 | tf_op jit(solution)/shard_map/all_gather | solution.py:107
  82.9 202.1 %reduce-scatter.3.cloned.1.call-start = ((), (), s32[]{:S(2)}) async-start(), calls=%async_computation.7 | async-start | bytes 2359296 | tf_op jit(solution)/shard_map/reduce_scatter | solution.py:102
  184.8 0.7 copy-start.4
  184.8 2.8 copy-start.6
  184.8 3.5 copy-start.9
  187.5 202.9 %reduce-scatter.5.cloned.1.call-start = ((), (), s32[]{:S(2)}) async-start(), calls=%async_computation.9 | async-start | bytes 2359296 | tf_op jit(solution)/shard_map/reduce_scatter | solution.py:111
  287.8 105.3 %all-to-all-start.2 = ((bf16[64,4,1024]{2,1,0:T(4,128)(2,1)}), bf16[64,4,1024]{2,1,0:T(4,128)(2,1)S(1)}, u32[]{:S(2)}, u32[]{:S(2)}) async-start(bf16[64,4,1024]{2,1,0:T(4,128)(2,1)} %reshape.208), calls=%async_computation.3 | async-start | bytes 1048576 | tf_op jit(solution)/shard_map/all_to_all | solution.py:105
  393.1 27.7 %all-to-all-start.4 = ((bf16[64,4,1024]{2,1,0:T(4,128)(2,1)}), bf16[64,4,1024]{2,1,0:T(4,128)(2,1)S(1)}, u32[]{:S(2)}, u32[]{:S(2)}) async-start(bf16[64,4,1024]{2,1,0:T(4,128)(2,1)} %reshape.211), calls=%async_computation.6 | async-start | bytes 1048576 | tf_op jit(solution)/shard_map/all_to_all | solution.py:114
  403.2 2.3 copy-start.7
  403.3 3.5 copy-start.3
  403.3 3.5 copy-start.5
Sparse Core Ops, SparseCore 0:
  86.8 95.3 all-gather.1
  187.7 97.3 reduce-scatter.2
  289.7 100.6 reduce-scatter.4
